TPU v7x, 32 devices: a whole 2x2x4 slice. The times are simulated.
32 devices in a mesh: rep: 8 (over y, x, core), fsdp: 4 (over z).
Axes of the slice: x: 2, y: 2, z: 4, core: 2. Of those that a mesh axis runs over, the one named last changes fastest.
Arguments:
- tokens: bfloat16 [4096, 4096], P('rep', 'fsdp'), may hold values from -6 to 6
- gate_weight: bfloat16 [4096, 7168], P('rep', 'fsdp'), may hold values from -0.09375 to 0.09375
- up_act: bfloat16 [4096, 7168], P('rep', 'fsdp'), may hold values from -6 to 6
- cotangent: bfloat16 [4096, 7168], P('rep', 'fsdp'), may hold values from -0.099609375 to 0.099609375
Outputs:
- grad_sum: bfloat16 [4096, 7168], P('rep', 'fsdp')
- curvature: float32 [7168], P('fsdp')
- spread: float32 [7168], P('fsdp')
All inputs are finite; a program needn't handle non-finite values.
Results may differ from a plain program's by a relative error of at most 0.024.
Values may be sent and summed in bfloat16 or wider, within the bound.
A program may use at most 128 MiB of HBM per device.

v0:
```python
import jax
import jax.numpy as jnp
from jax import lax
from jax.sharding import PartitionSpec as P


def shards(tokens, gate_weight, up_act, cotangent):
    features_all = lax.all_gather(tokens, "fsdp", axis=1, tiled=True)
    replicas = lax.axis_size("rep")

    def add_rows(block_rows):
        return jnp.dot(features_all, block_rows, preferred_element_type=jnp.float32)

    gate_pre = add_rows(lax.all_gather(gate_weight, "rep", axis=0, tiled=True))
    sigmoid_gate = jax.nn.sigmoid(gate_pre)
    deriv_one = sigmoid_gate * (1.0 + gate_pre * (1.0 - sigmoid_gate))
    deriv_two = sigmoid_gate * (1.0 - sigmoid_gate) * (2.0 + gate_pre * (1.0 - 2.0 * sigmoid_gate))
    weighted = cotangent.astype(jnp.float32) * up_act.astype(jnp.float32)
    token_coeff = (weighted * deriv_one).astype(jnp.bfloat16)
    bend_weight = weighted * deriv_two
    rep_grad = lax.dot_general(
        features_all, token_coeff, (((0,), (0,)), ((), ())), preferred_element_type=jnp.float32
    ).astype(jnp.bfloat16)
    own_proj = jnp.dot(features_all, rep_grad, preferred_element_type=jnp.float32)
    grad_shard = lax.psum_scatter(
        rep_grad.astype(jnp.float32).astype(jnp.bfloat16), "rep", scatter_dimension=0, tiled=True
    )
    mean_proj = add_rows(lax.all_gather(grad_shard, "rep", axis=0, tiled=True)) / replicas
    deviate = own_proj - mean_proj
    curv_part = jnp.sum(bend_weight * mean_proj * mean_proj, axis=0)
    spread_part = jnp.sum(bend_weight * deviate * deviate, axis=0)
    curvature, spread_total = lax.psum((curv_part, spread_part), "rep")
    return (grad_shard, curvature, spread_total / (replicas - 1))


def solution(mesh):
    placed = (P("rep", "fsdp"), P("rep", "fsdp"), P("rep", "fsdp"), P("rep", "fsdp"))
    return jax.shard_map(
        shards,
        mesh=mesh,
        in_specs=placed,
        out_specs=(P("rep", "fsdp"), P("fsdp"), P("fsdp")),
        check_vma=False,
    )
```

profile of v0, /device:TPU:0, one launch (start us, length us, event | category | flops | bytes accessed | tf_op | source)
XLA Modules:
  0.0 455.3 jit_solution(8435540799089013819)
XLA Ops:
  7.2 0.0 all-gather.4.cloned.1.call-start
  7.2 0.7 all-gather.4.cloned.1.call-update
  7.9 0.0 all-gather.6.cloned.1.call-start
  7.9 0.7 all-gather.6.cloned.1.call-update
  8.6 0.0 copy-start.2
  8.7 0.0 reduce-scatter.2.cloned.1.call-start
  8.7 84.3 %all-gather.4.cloned.1.call-done = bf16[512,4096]{1,0:T(8,128)(2,1)} async-done(((bf16[512,1024]{1,0:T(8,128)(2,1)}), bf16[512,4096]{1,0:T(8,128)(2,1)}) %all-gather.4.cloned.1.call-update) | async-done | bytes 4194320 | tf_op jit(solution)/shard_map/all_gather | solution.py:8
  93.0 81.3 %all-gather.6.cloned.1.call-done = bf16[4096,1792]{1,0:T(8,128)(2,1)} async-done(((bf16[512,1792]{1,0:T(8,128)(2,1)}), bf16[4096,1792]{1,0:T(8,128)(2,1)}) %all-gather.6.cloned.1.call-update) | async-done | bytes 14680080 | tf_op jit(solution)/shard_map/all_gather | solution.py:14
  174.3 16.7 %fusion.11 = f32[512,1792]{1,0:T(8,128)} fusion(bf16[512,4096]{1,0:T(8,128)(2,1)} %all-gather.4.cloned.1.call-done, bf16[4096,1792]{1,0:T(8,128)(2,1)} %all-gather.6.cloned.1.call-done), kind=kOutput, calls=%fused_computation.20 | convolution fusion | flops 7516192768 | bytes 22544384 | tf_op jit(solution)/shard_map/dot_general | solution.py:12
  191.0 0.0 copy-done.2
  191.0 0.0 copy-done
  191.0 0.0 copy-done.3
  191.0 15.3 %convolution_convert_fusion = bf16[1792,4096]{1,0:T(8,128)(2,1)} fusion(bf16[512,4096]{1,0:T(8,128)(2,1)S(1)} %copy-done, f32[512,1792]{1,0:T(8,128)} %fusion.11, bf16[512,1792]{1,0:T(8,128)(2,1)S(1)} %copy-done.2, bf16[512,1792]{1,0:T(8,128)(2,1)S(1)} %copy-done.3), kind=kOutput, calls=%fused_computation | convolution fusion | flops 7534542848 | bytes 26214400 | tf_op jit(solution)/shard_map/dot_general | solution.py:21
  206.3 0.0 reduce-scatter.2.cloned.1.call-update
  206.4 0.2 all-gather.8.cloned.1.call-start
  206.6 102.2 %reduce-scatter.2.cloned.1.call-done = bf16[512,1792]{0,1:T(8,128)(2,1)} async-done(((bf16[4096,1792]{0,1:T(8,128)(2,1)}), bf16[512,1792]{0,1:T(8,128)(2,1)}) %reduce-scatter.2.cloned.1.call-update) | async-done | bytes 1835024 | tf_op jit(solution)/shard_map/reduce_scatter | solution.py:25
  308.8 0.0 all-gather.8.cloned.1.call-update
  308.8 3.8 copy.7
  312.6 81.6 %all-gather.8.cloned.1.call-done = bf16[4096,1792]{0,1:T(8,128)(2,1)} async-done(((bf16[512,1792]{0,1:T(8,128)(2,1)}), bf16[4096,1792]{0,1:T(8,128)(2,1)}) %all-gather.8.cloned.1.call-update) | async-done | bytes 14680080 | tf_op jit(solution)/shard_map/all_gather | solution.py:28
  394.2 16.5 %fusion.6 = (f32[1792]{0:T(1024)S(1)}, f32[1792,512]{0,1:T(8,128)S(1)}) fusion(f32[512,1792]{1,0:T(8,128)} %fusion.11, bf16[512,1792]{1,0:T(8,128)(2,1)S(1)} %copy-done.2, bf16[512,1792]{1,0:T(8,128)(2,1)} %param.7, bf16[4096,1792]{0,1:T(8,128)(2,1)} %all-gather.8.cloned.1.call-done, bf16[512,4096]{1,0:T(8,128)(2,1)} %all-gather.4.cloned.1.call-done), kind=kOutput, calls=%fused_computation.11 | convolution fusion | flops 7532705792 | bytes 29891584 | tf_op jit(solution)/shard_map/dot_general | solution.py:12
  410.8 0.0 copy-done.1
  410.8 13.8 %fusion.7 = f32[1792]{0:T(1024)S(1)} fusion(f32[1792,512]{0,1:T(8,128)S(1)} %get-tuple-element.9, bf16[1792,4096]{1,0:T(8,128)(2,1)} %convolution_convert_fusion, bf16[512,4096]{1,0:T(8,128)(2,1)S(1)} %copy-done.1, f32[512,1792]{1,0:T(8,128)S(1)} %copy-done.5, bf16[512,1792]{1,0:T(8,128)(2,1)S(1)} %copy-done.2, bf16[512,1792]{1,0:T(8,128)(2,1)S(1)} %copy-done.4), kind=kOutput, calls=%fused_computation.12 | convolution fusion | flops 7532705792 | bytes 29891584 | tf_op jit(solution)/shard_map/dot_general | solution.py:24
  424.7 23.5 %all-reduce = (f32[1792]{0:T(1024)}, f32[1792]{0:T(1024)S(1)}) all-reduce(f32[1792]{0:T(1024)S(1)} %get-tuple-element.8, f32[1792]{0:T(1024)S(1)} %fusion.7), channel_id=1, replica_groups=mesh['rep'=8,'fsdp'=4] {'rep'}, use_global_device_ids=true, to_apply=%region_2.0 | all-reduce | flops 3584 | bytes 28672 | tf_op jit(solution)/shard_map/psum | solution.py:32
  448.1 0.6 broadcast_multiply_fusion
  (7 shorter events, 0.0 us)
Async XLA Ops:
  7.2 85.9 %all-gather.4.cloned.1.call-start = ((), (), s32[]{:S(2)}) async-start(), calls=%async_computation.1 | async-start | bytes 5242880 | tf_op jit(solution)/shard_map/all_gather | solution.py:8
  7.9 166.4 %all-gather.6.cloned.1.call-start = ((), (), s32[]{:S(2)}) async-start(), calls=%async_computation.2 | async-start | bytes 16515072 | tf_op jit(solution)/shard_map/all_gather | solution.py:14
  8.6 182.4 %copy-start.2 = (bf16[512,1792]{1,0:T(8,128)(2,1)S(1)}, bf16[512,1792]{1,0:T(8,128)(2,1)}, u32[]{:S(2)}) copy-start(bf16[512,1792]{1,0:T(8,128)(2,1)} %param.6) | copy-start | bytes 5505028
  8.7 300.1 %reduce-scatter.2.cloned.1.call-start = ((), (), s32[]{:S(2)}) async-start(), calls=%async_computation.3 | async-start | bytes 16515072 | tf_op jit(solution)/shard_map/reduce_scatter | solution.py:25
  174.3 16.7 %copy-start = (bf16[512,4096]{1,0:T(8,128)(2,1)S(1)}, bf16[512,4096]{1,0:T(8,128)(2,1)}, u32[]{:S(2)}) copy-start(bf16[512,4096]{1,0:T(8,128)(2,1)} %all-gather.4.cloned.1.call-done) | copy-start | bytes 12582916
  174.3 16.7 %copy-start.3 = (bf16[512,1792]{1,0:T(8,128)(2,1)S(1)}, bf16[512,1792]{1,0:T(8,128)(2,1)}, u32[]{:S(2)}) copy-start(bf16[512,1792]{1,0:T(8,128)(2,1)} %param.7) | copy-start | bytes 5505028
  206.4 187.9 %all-gather.8.cloned.1.call-start = ((), (), s32[]{:S(2)}) async-start(), calls=%async_computation.4 | async-start | bytes 16515072 | tf_op jit(solution)/shard_map/all_gather | solution.py:28
  394.2 16.5 %copy-start.1 = (bf16[512,4096]{1,0:T(8,128)(2,1)S(1)}, bf16[512,4096]{1,0:T(8,128)(2,1)}, u32[]{:S(2)}) copy-start(bf16[512,4096]{1,0:T(8,128)(2,1)} %all-gather.4.cloned.1.call-done) | copy-start | bytes 12582916
  394.2 16.6 %copy-start.4 = (bf16[512,1792]{1,0:T(8,128)(2,1)S(1)}, bf16[512,1792]{1,0:T(8,128)(2,1)}, u32[]{:S(2)}) copy-start(bf16[512,1792]{1,0:T(8,128)(2,1)} %param.7) | copy-start | bytes 5505028
  394.2 16.6 %copy-start.5 = (f32[512,1792]{1,0:T(8,128)S(1)}, f32[512,1792]{1,0:T(8,128)}, u32[]{:S(2)}) copy-start(f32[512,1792]{1,0:T(8,128)} %fusion.11) | copy-start | bytes 11010052
Sparse Core Ops, SparseCore 0:
  9.5 83.4 all-gather.3
  94.9 79.3 all-gather.5
  206.5 102.2 reduce-scatter.1
  310.5 83.7 all-gather.7
where the time goes:
time: 456 us; the launch traced here: 455 us
  waiting for transfers between devices  351 us (77%)
  matrix products  62.4 us (14%)
  blocking collectives  23.5 us (5%)
  between operations  13.8 us (3%)
    reduce_scatter x1, waiting for transfers between devices, shards(): lax.psum_scatter(rep_grad.astype(jnp.float32).astype(jnp.bfloat16), 'rep'...  102 us
    all_gather x1, waiting for transfers between devices, shards(): features_all = lax.all_gather(tokens, 'fsdp', axis=1, tiled=True)  84.3 us
    all_gather x1, waiting for transfers between devices, shards(): lax.all_gather(grad_shard, 'rep', axis=0, tiled=True)  81.6 us
    all_gather x1, waiting for transfers between devices, shards(): gate_pre = add_rows(lax.all_gather(gate_weight, 'rep', axis=0, tiled=True))  81.3 us
    dot_general x2, matrix products, add_rows(): return jnp.dot(features_all, block_rows, preferred_element_type=jnp.float32)  33.2 us
    psum x1, blocking collectives, shards(): curvature, spread_total = lax.psum((curv_part, spread_part), 'rep')  23.5 us
    dot_general x1, matrix products, shards(): lax.dot_general(features_all, token_coeff, (((0,), (0,)), ((), ())), pref...  15.3 us
    dot_general x1, matrix products, shards(): jnp.dot(features_all, rep_grad, preferred_element_type=jnp.float32)  13.8 us
  transfers between devices with their start and end apart: 4, of which 4 were waited for; matrix products, arithmetic and copies ran while one was open for 1% of the time, Pallas kernels for 0%

commit v1 on v0

--- a/solution.py
+++ b/solution.py
@@ -5,7 +5,12 @@
 
 
 def shards(tokens, gate_weight, up_act, cotangent):
-    features_all = lax.all_gather(tokens, "fsdp", axis=1, tiled=True)
+    ring = [tokens]
+    for hop in range(3):
+        ring.append(lax.ppermute(ring[-1], "fsdp", [(dev, (dev + 1) % 4) for dev in range(4)]))
+    features_all = jnp.roll(
+        jnp.concatenate(ring[::-1], axis=1), (lax.axis_index("fsdp") + 1) * ring[0].shape[1], axis=1
+    )
     replicas = lax.axis_size("rep")
 
     def add_rows(block_rows):

time: 456 us -> 376 us (0.82)
  waiting for transfers between devices: 351 us -> 263 us
  local copies, waits for them, and re-layouts: 3.83 us -> 13.5 us
    all_gather x1 -> x0, waiting for transfers between devices: 84.3 us -> none  [shards(): features_all = lax.all_gather(tokens, 'fsdp', axis=1, tiled=True)]
    all_gather x1, waiting for transfers between devices: 81.3 us -> 0.01 us  [shards(): gate_pre = add_rows(lax.all_gather(gate_weight, 'rep', axis=0, tiled=True))]
    ppermute x0 -> x3, waiting for transfers between devices: none -> 76.9 us  [shards(): lax.ppermute(ring[-1], 'fsdp', [(dev, (dev + 1) % 4) for dev in range(4)])]
    unnamed x13 -> x19, local copies, waits for them, and re-layouts: 3.83 us -> 12.3 us
    dot_general x2, matrix products: 33.2 us -> 28.2 us  [add_rows(): return jnp.dot(features_all, block_rows, preferred_element_type=jnp.float32)]
  transfers between devices with their start and end apart: 4 -> 6, of which waited for: 4 -> 5; matrix products, arithmetic and copies ran while one was open for 1% -> 3% of each run, Pallas kernels for 0% -> 0%
where the time goes in v1:
time: 376 us
  waiting for transfers between devices  263 us (70%)
  matrix products  58 us (15%)
  blocking collectives  23.5 us (6%)
  between operations  13.8 us (4%)
  local copies, waits for them, and re-layouts  13.5 us (4%)
    reduce_scatter x1, waiting for transfers between devices, shards(): lax.psum_scatter(rep_grad.astype(jnp.float32).astype(jnp.bfloat16), 'rep'...  102 us
    all_gather x1, waiting for transfers between devices, shards(): lax.all_gather(grad_shard, 'rep', axis=0, tiled=True)  83.3 us
    ppermute x3, waiting for transfers between devices, shards(): lax.ppermute(ring[-1], 'fsdp', [(dev, (dev + 1) % 4) for dev in range(4)])  76.9 us
    dot_general x2, matrix products, add_rows(): return jnp.dot(features_all, block_rows, preferred_element_type=jnp.float32)  28.2 us
    psum x1, blocking collectives, shards(): curvature, spread_total = lax.psum((curv_part, spread_part), 'rep')  23.5 us
    dot_general x1, matrix products, shards(): jnp.dot(features_all, rep_grad, preferred_element_type=jnp.float32)  15 us
    dot_general x1, matrix products, shards(): lax.dot_general(features_all, token_coeff, (((0,), (0,)), ((), ())), pref...  14.8 us
    unnamed x19, local copies, waits for them, and re-layouts  12.3 us
  transfers between devices with their start and end apart: 6, of which 5 were waited for; matrix products, arithmetic and copies ran while one was open for 3% of the time, Pallas kernels for 0%

profile of v1, /device:TPU:0, one launch (start us, length us, event | category | flops | bytes accessed | tf_op | source)
XLA Modules:
  0.0 376.0 jit_solution(3544414058344754333)
XLA Ops:
  7.2 0.7 all-gather.3.cloned.1.call-update
  7.9 0.0 reduce-scatter.2.cloned.1.call-start
  8.0 3.1 collective-permute-start
  11.1 25.4 %collective-permute-done = bf16[512,1024]{1,0:T(8,128)(2,1)S(1)} collective-permute-done((bf16[512,1024]{1,0:T(8,128)(2,1)}, bf16[512,1024]{1,0:T(8,128)(2,1)S(1)}, u32[]{:S(2)}, u32[]{:S(2)}) %collective-permute-start) | collective-permute-done | bytes 1048608 | tf_op jit(solution)/shard_map/ppermute | solution.py:10
  36.5 26.1 %collective-permute-done.1 = bf16[512,1024]{1,0:T(8,128)(2,1)S(1)} collective-permute-done((bf16[512,1024]{1,0:T(8,128)(2,1)S(1)}, bf16[512,1024]{1,0:T(8,128)(2,1)S(1)}, u32[]{:S(2)}, u32[]{:S(2)}) %collective-permute-start.1) | collective-permute-done | bytes 1048608 | tf_op jit(solution)/shard_map/ppermute | solution.py:10
  62.6 25.4 %collective-permute-done.2 = bf16[512,1024]{1,0:T(8,128)(2,1)} collective-permute-done((bf16[512,1024]{1,0:T(8,128)(2,1)S(1)}, bf16[512,1024]{1,0:T(8,128)(2,1)}, u32[]{:S(2)}, u32[]{:S(2)}) %collective-permute-start.2) | collective-permute-done | bytes 1048608 | tf_op jit(solution)/shard_map/ppermute | solution.py:10
  87.9 2.4 constant_dynamic-update-slice_fusion.7
  90.4 1.1 constant_dynamic-update-slice_fusion.6
  91.5 1.1 constant_dynamic-update-slice_fusion.5
  92.6 1.2 constant_dynamic-update-slice_fusion.4
  93.8 2.4 constant_dynamic-update-slice_fusion.3
  96.2 1.2 constant_dynamic-update-slice_fusion.2
  97.3 1.1 constant_dynamic-update-slice_fusion.1
  98.5 1.2 constant_dynamic-update-slice_fusion
  99.7 11.8 %fusion.12 = f32[512,1792]{1,0:T(8,128)S(1)} fusion(bf16[4096,1792]{1,0:T(8,128)(2,1)} %all-gather.3.cloned.1.call-done, bf16[512,8192]{1,0:T(8,128)(2,1)} %constant_dynamic-update-slice_fusion, s32[]{:T(128)S(6)} %select_n.14), kind=kOutput, calls=%fused_computation.19 | convolution fusion | flops 7516192768 | bytes 22544388 | tf_op jit(solution)/shard_map/dot_general | solution.py:17
  111.5 1.8 copy-done.4
  113.3 14.8 %convolution_convert_fusion = bf16[4096,1792]{1,0:T(8,128)(2,1)} fusion(bf16[512,8192]{1,0:T(8,128)(2,1)} %constant_dynamic-update-slice_fusion, s32[]{:T(128)S(6)} %select_n.14, f32[512,1792]{1,0:T(8,128)S(1)} %fusion.12, bf16[512,1792]{1,0:T(8,128)(2,1)S(1)} %copy-done.1, bf16[512,1792]{1,0:T(8,128)(2,1)S(1)} %copy-done.2), kind=kOutput, calls=%fused_computation | convolution fusion | flops 7534542848 | bytes 26214404 | tf_op jit(solution)/shard_map/dot_general | solution.py:26
  128.1 0.2 all-gather.5.cloned.1.call-start
  128.3 102.3 %reduce-scatter.2.cloned.1.call-done = bf16[512,1792]{1,0:T(8,128)(2,1)} async-done(((bf16[4096,1792]{1,0:T(8,128)(2,1)}), bf16[512,1792]{1,0:T(8,128)(2,1)}) %reduce-scatter.2.cloned.1.call-update) | async-done | bytes 1835024 | tf_op jit(solution)/shard_map/reduce_scatter | solution.py:30
  230.6 83.3 %all-gather.5.cloned.1.call-done = bf16[4096,1792]{1,0:T(8,128)(2,1)} async-done(((bf16[512,1792]{1,0:T(8,128)(2,1)}), bf16[4096,1792]{1,0:T(8,128)(2,1)}) %all-gather.5.cloned.1.call-update) | async-done | bytes 14680080 | tf_op jit(solution)/shard_map/all_gather | solution.py:33
  314.0 16.3 %fusion.6 = (f32[1792]{0:T(1024)S(1)}, f32[512,1792]{1,0:T(8,128)S(1)}) fusion(f32[512,1792]{1,0:T(8,128)} %copy-done.4, bf16[512,1792]{1,0:T(8,128)(2,1)S(1)} %copy-done.1, bf16[512,1792]{1,0:T(8,128)(2,1)} %param.7, bf16[4096,1792]{1,0:T(8,128)(2,1)} %all-gather.5.cloned.1.call-done, bf16[512,8192]{1,0:T(8,128)(2,1)} %constant_dynamic-update-slice_fusion, ...), kind=kOutput, calls=%fused_computation.11 | convolution fusion | flops 7532705792 | bytes 29891588 | tf_op jit(solution)/shard_map/dot_general | solution.py:17
  330.4 15.0 %fusion.7 = f32[1792]{0:T(1024)S(1)} fusion(f32[512,1792]{1,0:T(8,128)S(1)} %get-tuple-element.6, bf16[4096,1792]{1,0:T(8,128)(2,1)} %convolution_convert_fusion, bf16[512,8192]{1,0:T(8,128)(2,1)} %constant_dynamic-update-slice_fusion, s32[]{:T(128)S(6)} %select_n.14, f32[512,1792]{1,0:T(8,128)S(1)} %copy-done.5, bf16[512,1792]{1,0:T(8,128)(2,1)S(1)} %copy-done.1, ...), kind=kOutput, calls=%fused_computation.12 | convolution fusion | flops 7533623296 | bytes 29891588 | tf_op jit(solution)/shard_map/dot_general | solution.py:29
  345.4 23.5 %all-reduce = (f32[1792]{0:T(1024)}, f32[1792]{0:T(1024)S(1)}) all-reduce(f32[1792]{0:T(1024)S(1)} %get-tuple-element.5, f32[1792]{0:T(1024)S(1)} %fusion.7), channel_id=1, replica_groups=mesh['rep'=8,'fsdp'=4] {'rep'}, use_global_device_ids=true, to_apply=%region_2.3 | all-reduce | flops 3584 | bytes 28672 | tf_op jit(solution)/shard_map/psum | solution.py:37
  368.9 0.6 broadcast_multiply_fusion
  (17 shorter events, 0.1 us)
Async XLA Ops:
  7.2 85.5 %copy-start = (bf16[512,1024]{1,0:T(8,128)(2,1)S(1)}, bf16[512,1024]{1,0:T(8,128)(2,1)}, u32[]{:S(2)}) copy-start(bf16[512,1024]{1,0:T(8,128)(2,1)} %param.4) | copy-start | bytes 3145732
  7.2 92.5 %all-gather.3.cloned.1.call-start = ((), (), s32[]{:S(2)}) async-start(), calls=%async_computation.1 | async-start | bytes 16515072 | tf_op jit(solution)/shard_map/all_gather | solution.py:19
  7.9 222.7 %reduce-scatter.2.cloned.1.call-start = ((), (), s32[]{:S(2)}) async-start(), calls=%async_computation.2 | async-start | bytes 16515072 | tf_op jit(solution)/shard_map/reduce_scatter | solution.py:30
  8.0 28.5 %collective-permute-start = (bf16[512,1024]{1,0:T(8,128)(2,1)}, bf16[512,1024]{1,0:T(8,128)(2,1)S(1)}, u32[]{:S(2)}, u32[]{:S(2)}) collective-permute-start(bf16[512,1024]{1,0:T(8,128)(2,1)} %param.4), channel_id=1, source_target_pairs={{0,1},{1,2},{2,3},{3,0},{4,5},{5,6},{6,7},{7,4},{8,9},{9,10},{10,1... | collective-permute-start | bytes 3145736 | tf_op jit(solution)/shard_map/ppermute | solution.py:10
  36.5 26.1 %collective-permute-start.1 = (bf16[512,1024]{1,0:T(8,128)(2,1)S(1)}, bf16[512,1024]{1,0:T(8,128)(2,1)S(1)}, u32[]{:S(2)}, u32[]{:S(2)}) collective-permute-start(bf16[512,1024]{1,0:T(8,128)(2,1)S(1)} %collective-permute-done), channel_id=1, source_target_pairs={{0,1},{1,2},{2,3},{3,0},{4,5},{5,6},{6,7},{7,4},{8,9},{9,10},{10,1... | collective-permute-start | bytes 3145736 | tf_op jit(solution)/shard_map/ppermute | solution.py:10
  62.6 25.4 %collective-permute-start.2 = (bf16[512,1024]{1,0:T(8,128)(2,1)S(1)}, bf16[512,1024]{1,0:T(8,128)(2,1)}, u32[]{:S(2)}, u32[]{:S(2)}) collective-permute-start(bf16[512,1024]{1,0:T(8,128)(2,1)S(1)} %collective-permute-done.1), channel_id=1, source_target_pairs={{0,1},{1,2},{2,3},{3,0},{4,5},{5,6},{6,7},{7,4},{8,9},{9,10},{10,1... | collective-permute-start | bytes 3145736 | tf_op jit(solution)/shard_map/ppermute | solution.py:10
  99.7 13.6 %copy-start.1 = (bf16[512,1792]{1,0:T(8,128)(2,1)S(1)}, bf16[512,1792]{1,0:T(8,128)(2,1)}, u32[]{:S(2)}) copy-start(bf16[512,1792]{1,0:T(8,128)(2,1)} %param.6) | copy-start | bytes 5505028
  99.7 13.6 %copy-start.2 = (bf16[512,1792]{1,0:T(8,128)(2,1)S(1)}, bf16[512,1792]{1,0:T(8,128)(2,1)}, u32[]{:S(2)}) copy-start(bf16[512,1792]{1,0:T(8,128)(2,1)} %param.7) | copy-start | bytes 5505028
  111.5 1.8 copy-start.4
  128.1 185.9 %all-gather.5.cloned.1.call-start = ((), (), s32[]{:S(2)}) async-start(), calls=%async_computation.3 | async-start | bytes 16515072 | tf_op jit(solution)/shard_map/all_gather | solution.py:33
  314.0 16.4 %copy-start.3 = (bf16[512,1792]{1,0:T(8,128)(2,1)S(1)}, bf16[512,1792]{1,0:T(8,128)(2,1)}, u32[]{:S(2)}) copy-start(bf16[512,1792]{1,0:T(8,128)(2,1)} %param.7) | copy-start | bytes 5505028
  314.0 16.4 %copy-start.5 = (f32[512,1792]{1,0:T(8,128)S(1)}, f32[512,1792]{1,0:T(8,128)}, u32[]{:S(2)}) copy-start(f32[512,1792]{1,0:T(8,128)} %copy-done.4) | copy-start | bytes 11010052
Sparse Core Ops, SparseCore 0:
  9.9 83.5 all-gather.2
  128.2 102.3 reduce-scatter.1
  233.1 80.8 all-gather.4
